TPU v7x, 32 devices: a whole 2x2x4 slice. The times are simulated.
32 devices in a mesh: node: 4 (over z), band: 8 (over y, x, core).
Axes of the slice: x: 2, y: 2, z: 4, core: 2. Of those that a mesh axis runs over, the one named last changes fastest.
Arguments:
- state0: float32 [2, 1024, 4, 3, 512], P(None, 'band'), may hold values from -36 to 36
- iterate: float32 [4, 2, 1024, 4, 3, 512], P('node', None, 'band'), may hold values from -37.2 to 37.2
- legendre: bfloat16 [1024, 512, 512], P('band'), may hold values from -0.25 to 0.25
- lat_weight: float32 [512], replicated, may hold values from 0.25 to 1
- coriolis: float32 [2, 512], replicated, may hold values from -1.5 to 1.5
- damping: float32 [1024, 3, 512], P('band'), may hold values from 0.1 to 10
- quadrature: float32 [4, 4], replicated, may hold values from 0.02 to 0.25
Outputs:
- updated: float32 [4, 2, 1024, 4, 3, 512], P('node', None, 'band')
- sweep_change: float32 [3], replicated
All inputs are finite; a program needn't handle non-finite values.
Results may differ from a plain program's by a relative error of at most 0.0017.
Values may be sent and summed in bfloat16 or wider, within the bound.
A program may use at most 256 MiB of HBM per device.

v0:
```python
import math

import jax
import jax.numpy as jnp
from jax import lax
from jax.sharding import PartitionSpec as P


def transform_tables(modes, points):
    wave = lax.iota(jnp.int32, modes)
    cell = lax.iota(jnp.int32, points)
    phase = wave[:, None] * cell[None, :] % points
    angle = phase.astype(jnp.float32) * (2.0 * math.pi / points)
    cosine = jnp.cos(angle)
    sine = jnp.sin(angle)
    scale = 1.0 / math.sqrt(modes)
    ratio = (wave.astype(jnp.float32) / modes)[:, None]
    forward = jnp.stack([cosine, -sine], axis=0) * scale
    slope_table = jnp.stack([-ratio * sine, -ratio * cosine], axis=0) * scale
    backward = jnp.stack([forward, slope_table], axis=2)
    return (forward, backward)


def body(state0, iterate, legendre, lat_weight, coriolis, damping, quadrature):
    base_total = lax.psum(jnp.sum(state0 * state0, axis=(0, 1, 2, 4)), "band")
    spec = iterate[0]
    half = legendre.shape[2] // 2
    local_modes = legendre.shape[0]
    hemi = legendre.shape[1]
    members = spec.shape[2]
    nband = lax.axis_size("band")
    nnode = lax.axis_size("node")
    modes = local_modes * nband
    points = 2 * modes
    node = lax.axis_index("node")
    band = lax.axis_index("band")
    forward, backward = transform_tables(modes, points)
    coeff = spec.astype(jnp.bfloat16)
    even = jnp.einsum(
        "cmefj,mlj->cmefl",
        coeff[..., :half],
        legendre[:, :, :half],
        preferred_element_type=jnp.float32,
    )
    odd = jnp.einsum(
        "cmefj,mlj->cmefl",
        coeff[..., half:],
        legendre[:, :, half:],
        preferred_element_type=jnp.float32,
    )
    groups = 1
    even_grid, odd_grid = (
        lax.all_to_all(even, "band", split_axis=4, concat_axis=1, tiled=True),
        lax.all_to_all(odd, "band", split_axis=4, concat_axis=1, tiled=True),
    )
    lat_rows = hemi // (groups * nband)
    first = band * lat_rows
    even_grid = even_grid.reshape(2, groups, modes, members, 3, lat_rows)
    odd_grid = odd_grid.reshape(2, groups, modes, members, 3, lat_rows)
    fourier = jnp.stack([even_grid + odd_grid, even_grid - odd_grid], axis=5)
    grid = lax.dot_general(
        fourier, backward, (((0, 2), (0, 1)), ((), ())), precision=lax.Precision.HIGHEST
    )
    values = grid[..., 0, :]
    slopes = grid[..., 1, :]
    cor = lax.dynamic_slice_in_dim(coriolis, first, lat_rows, 1)[:, :, None]
    weight = lax.dynamic_slice_in_dim(lat_weight, first, lat_rows, 0)
    u_wind, v_wind, height = (values[:, :, 0], values[:, :, 1], values[:, :, 2])
    u_slope, v_slope, h_slope = (slopes[:, :, 0], slopes[:, :, 1], slopes[:, :, 2])
    tend_u = -u_wind * u_slope + cor * v_wind - h_slope
    tend_v = -u_wind * v_slope - cor * u_wind
    tend_h = -u_wind * h_slope - (1.0 + height) * u_slope
    tend = jnp.stack([tend_u, tend_v, tend_h], axis=2)
    spectra = jnp.einsum("cmk,qefhlk->cqmefhl", forward, tend, precision=lax.Precision.HIGHEST)
    symmetric = (weight * (spectra[..., 0, :] + spectra[..., 1, :])).astype(jnp.bfloat16)
    antisymmetric = (weight * (spectra[..., 0, :] - spectra[..., 1, :])).astype(jnp.bfloat16)
    symmetric = symmetric.reshape(2, groups * modes, members, 3, lat_rows)
    antisymmetric = antisymmetric.reshape(2, groups * modes, members, 3, lat_rows)
    sym_spec, anti_spec = (
        lax.all_to_all(symmetric, "band", split_axis=1, concat_axis=4, tiled=True),
        lax.all_to_all(antisymmetric, "band", split_axis=1, concat_axis=4, tiled=True),
    )
    spec_even = jnp.einsum(
        "cmefl,mlj->cmefj", sym_spec, legendre[:, :, :half], preferred_element_type=jnp.float32
    )
    spec_odd = jnp.einsum(
        "cmefl,mlj->cmefj", anti_spec, legendre[:, :, half:], preferred_element_type=jnp.float32
    )
    nonlinear = jnp.concatenate([spec_even, spec_odd], axis=-1)
    rate = damping[None, :, None]
    force = nonlinear - rate * spec
    quad_column = lax.dynamic_slice_in_dim(quadrature, node, 1, 1)[:, 0]
    mixed = lax.psum_scatter(
        quad_column[:, None, None, None, None, None] * force[None],
        "node",
        scatter_dimension=0,
        tiled=True,
    )[0]
    diag = lax.dynamic_slice(quadrature, (node, node), (1, 1))[0, 0]
    updated = (state0 + mixed + diag * rate * spec) / (1.0 + diag * rate)
    change = jnp.sum((updated - spec) ** 2, axis=(0, 1, 2, 4))
    total = lax.psum(change, ("node", "band"))
    ratio = jnp.sqrt(total / (nnode * base_total + 1e-06))
    return (updated[None], ratio)


def solution(mesh):
    placed = (
        P(None, "band", None, None, None),
        P("node", None, "band", None, None, None),
        P("band", None, None),
        P(),
        P(),
        P("band", None, None),
        P(),
    )
    return jax.shard_map(
        body,
        mesh=mesh,
        in_specs=placed,
        out_specs=(P("node", None, "band", None, None, None), P()),
        check_vma=False,
    )
```

profile of v0, /device:TPU:0, one launch (start us, length us, event | category | flops | bytes accessed | tf_op | source)
XLA Modules:
  0.0 1212.9 jit_solution(15115340711439680744)
XLA Ops:
  11.1 18.0 %fusion.60 = f32[2,128,4,3,512]{4,2,3,0,1:T(4,128)} fusion(bf16[128,512,512]{2,1,0:T(8,128)(2,1)} %param.9, bf16[2,128,4,3,512]{4,2,3,0,1:T(4,128)(2,1)S(1)} %bitcast.194), kind=kOutput, calls=%fused_computation.83 | convolution fusion | flops 805306368 | bytes 41418752 | tf_op jit(solution)/shard_map/cmefj,mlj->cmefl/dot_general | solution.py:39
  43.1 17.9 %fusion.57 = f32[2,128,4,3,512]{4,2,3,0,1:T(4,128)} fusion(bf16[128,512,512]{2,1,0:T(8,128)(2,1)} %param.9, bf16[2,128,4,3,512]{4,2,3,0,1:T(4,128)(2,1)S(1)} %bitcast.195), kind=kOutput, calls=%fused_computation.82 | convolution fusion | flops 805306368 | bytes 41418752 | tf_op jit(solution)/shard_map/cmefj,mlj->cmefl/dot_general | solution.py:45
  69.9 45.0 %all-to-all-done = f32[2,128,4,3,512]{1,2,3,0,4:T(4,128)} async-done(((f32[2,128,4,3,512]{1,2,3,0,4:T(4,128)}), f32[2,128,4,3,512]{1,2,3,0,4:T(4,128)}, u32[]{:S(2)}, u32[]{:S(2)}) %all-to-all-start) | async-done | bytes 6291488 | tf_op jit(solution)/shard_map/all_to_all | solution.py:53
  121.3 33.7 %multiply_bitcast_fusion.1 = (f32[1,1024,1,2048]{3,1,2,0:T(8,128)S(1)}, f32[1,1024,1,2048]{3,1,2,0:T(8,128)S(1)}) fusion(f32[1024]{0:T(1024)S(1)} %multiply_negate_fusion), kind=kLoop, calls=%fused_computation.44 | loop fusion | flops 33554432 | bytes 16781312 | tf_op jit(solution)/shard_map/stack | solution.py:19
  161.1 33.2 %fusion.55 = (f32[1,1024,1,2048]{3,1,0,2:T(8,128)S(1)}, f32[1,1024,1,2048]{3,1,0,2:T(8,128)S(1)}) fusion(), kind=kLoop, calls=%fused_computation.79 | loop fusion | flops 31457280 | bytes 16777216 | tf_op jit(solution)/shard_map/stack | solution.py:18
  200.4 34.6 %fusion.53 = (f32[1,1024,2048]{2,1,0:T(8,128)}, f32[1,1024,2048]{2,1,0:T(8,128)}) fusion(), kind=kLoop, calls=%fused_computation.77 | loop fusion | flops 31457280 | bytes 16777216 | tf_op jit(solution)/shard_map/cos | solution.py:14
  235.1 9.3 copy_add_fusion
  259.6 10.9 copy.113
  277.6 166.8 %fusion.27 = f32[1,4,3,2,64,2,2048]{6,4,5,3,2,1,0:T(8,128)} fusion(f32[2,1024,1,2048]{3,1,0,2:T(8,128)} %fusion.15, f32[2,1024,1,2048]{3,1,0,2:T(8,128)} %maximum_multiply_fusion, f32[2,1,1024,4,3,1,64]{2,6,0,5,4,3,1:T(8,128)} %sub.58, f32[2,1,1024,4,3,1,64]{2,6,0,5,4,3,1:T(8,128)} %add.140), kind=kOutput, calls=%fused_computation.38 | convolution fusion | flops 154630356992 | bytes 71303168 | tf_op jit(solution)/shard_map/dot_general | solution.py:61
  444.4 14.2 %slice_bitcast_fusion = (f32[1,4,3,2,64,2048]{5,4,3,2,1,0:T(8,128)S(1)}, f32[1,4,3,2,64,2048]{5,4,3,2,1,0:T(8,128)}) fusion(f32[1,4,3,2,64,2,2048]{6,4,5,3,2,1,0:T(8,128)} %fusion.27), kind=kLoop, calls=%fused_computation.24 | loop fusion | bytes 50331648 | tf_op jit(solution)/shard_map/squeeze | solution.py:65
  466.4 85.2 %fusion.44 = f32[2,1,1024,4,3,2,64]{2,6,0,5,4,3,1:T(8,128)} fusion(f32[1,1024,2048]{2,1,0:T(8,128)} %get-tuple-element.30, f32[1,1024,2048]{2,1,0:T(8,128)} %get-tuple-element.29, f32[1,4,1,2,64,2048]{5,4,3,2,1,0:T(8,128)} %get-tuple-element.18, f32[1,4,1,2,64,2048]{5,4,3,2,1,0:T(8,128)} %get-tuple-element.17, ...), kind=kOutput, calls=%fused_computation.67 | convolution fusion | flops 77324091392 | bytes 41943040 | tf_op jit(solution)/shard_map/cmk,qefhlk->cqmefhl/dot_general | solution.py:74
  558.8 11.1 copy.124
  569.9 9.1 reshape.336
  583.1 15.6 %copy.119 = bf16[2,1024,4,3,64]{4,0,3,2,1:T(2,128)(2,1)} copy(bf16[2,1024,4,3,64]{1,4,0,3,2:T(8,128)(2,1)} %get-tuple-element.21) | data formatting | bytes 6291456 | tf_op jit(solution)/shard_map/convert_element_type | solution.py:75
  607.7 13.3 %all-to-all-done.3 = bf16[8,2,98304]{2,1,0:T(2,128)(2,1)S(1)} async-done(((bf16[8,2,98304]{2,1,0:T(2,128)(2,1)}), bf16[8,2,98304]{2,1,0:T(2,128)(2,1)S(1)}, u32[]{:S(2)}, u32[]{:S(2)}) %all-to-all-start.3) | async-done | bytes 3145760 | tf_op jit(solution)/shard_map/all_to_all | solution.py:81
  634.5 13.7 %copy.146 = bf16[2,8,128,4,3,64]{2,5,1,4,3,0:T(8,128)(2,1)S(1)} copy(bf16[2,8,128,4,3,64]{5,0,4,3,2,1:T(2,128)(2,1)} %bitcast.187) | data formatting | bytes 6291456 | tf_op jit(solution)/shard_map/all_to_all | solution.py:81
  652.3 15.4 %fusion.63 = f32[1,2,128,4,3,256]{5,3,4,1,2,0:T(4,128)} fusion(bf16[2,128,4,3,512]{4,2,3,0,1:T(4,128)(2,1)} %copy.127, bf16[128,512,512]{2,1,0:T(8,128)(2,1)} %param.9), kind=kOutput, calls=%fused_computation.84 | convolution fusion | flops 805306368 | bytes 39845888 | tf_op jit(solution)/shard_map/cmefl,mlj->cmefj/dot_general | solution.py:86
  676.5 15.3 %copy.144 = bf16[2,8,128,4,3,64]{2,5,1,4,3,0:T(8,128)(2,1)} copy(bf16[2,8,128,4,3,64]{5,0,4,3,2,1:T(2,128)(2,1)} %bitcast.188) | data formatting | bytes 6291456 | tf_op jit(solution)/shard_map/all_to_all | solution.py:80
  698.1 16.0 %fusion.66 = f32[1,2,128,4,3,256]{5,3,4,1,2,0:T(4,128)} fusion(bf16[2,128,4,3,512]{4,2,3,0,1:T(4,128)(2,1)} %copy.122, bf16[128,512,512]{2,1,0:T(8,128)(2,1)} %param.9), kind=kOutput, calls=%fused_computation.85 | convolution fusion | flops 805306368 | bytes 39845888 | tf_op jit(solution)/shard_map/cmefl,mlj->cmefj/dot_general | solution.py:83
  722.3 9.3 broadcast_multiply_fusion
  736.1 14.7 %psum.15 = f32[3]{0:T(128)S(1)} all-reduce(f32[3]{0:T(128)S(1)} %multiply_reduce_fusion), channel_id=1, replica_groups=mesh['node'=4,'band'=8] {'band'}, use_global_device_ids=true, to_apply=%region_4.5 | all-reduce | flops 3 | bytes 24 | tf_op jit(solution)/shard_map/psum | solution.py:25
  753.4 395.1 %reduce-scatter.2.cloned.1.call-done = f32[1,2,128,4,3,512]{5,2,4,3,1,0:T(8,128)} async-done(((f32[4,2,128,4,3,512]{5,2,4,3,1,0:T(8,128)}), f32[1,2,128,4,3,512]{5,2,4,3,1,0:T(8,128)}) %reduce-scatter.2.cloned.1.call-update) | async-done | bytes 6291472 | tf_op jit(solution)/shard_map/reduce_scatter | solution.py:93
  1148.5 10.8 fusion.43
  1163.1 42.1 %psum.14 = f32[3]{0:T(128)S(1)} all-reduce(f32[3]{0:T(128)S(1)} %get-tuple-element.12), channel_id=1, replica_groups=mesh['node'=4,'band'=8] {'node','band'}, use_global_device_ids=true, to_apply=%region_2.3 | all-reduce | flops 3 | bytes 24 | tf_op jit(solution)/shard_map/psum | solution.py:102
  (56 shorter events, 147.8 us)
Async XLA Ops:
  7.2 114.1 %copy-start = (f32[2,512]{1,0:T(2,128)S(1)}, f32[2,512]{1,0:T(2,128)}, u32[]{:S(2)}) copy-start(f32[2,512]{1,0:T(2,128)} %param.11) | copy-start | bytes 12292
  37.9 77.0 %all-to-all-start = ((f32[2,128,4,3,512]{1,2,3,0,4:T(4,128)}), f32[2,128,4,3,512]{1,2,3,0,4:T(4,128)}, u32[]{:S(2)}, u32[]{:S(2)}) async-start(f32[2,128,4,3,512]{1,2,3,0,4:T(4,128)} %copy.106), calls=%async_computation | async-start | bytes 12582912 | tf_op jit(solution)/shard_map/all_to_all | solution.py:53
  115.0 120.1 %all-to-all-start.1 = ((f32[2,128,4,3,512]{1,2,3,0,4:T(4,128)}), f32[2,128,4,3,512]{1,2,3,0,4:T(4,128)}, u32[]{:S(2)}, u32[]{:S(2)}) async-start(f32[2,128,4,3,512]{1,2,3,0,4:T(4,128)} %copy.107), calls=%async_computation.1 | async-start | bytes 12582912 | tf_op jit(solution)/shard_map/all_to_all | solution.py:54
  466.4 85.2 %copy-start.6 = (f32[64]{0:T(128)S(1)}, f32[64]{0:T(128)}, u32[]{:S(2)}) copy-start(f32[64]{0:T(128)} %dynamic_slice.13) | copy-start | bytes 772
  579.0 42.0 %all-to-all-start.3 = ((bf16[8,2,98304]{2,1,0:T(2,128)(2,1)}), bf16[8,2,98304]{2,1,0:T(2,128)(2,1)S(1)}, u32[]{:S(2)}, u32[]{:S(2)}) async-start(bf16[8,2,98304]{2,1,0:T(2,128)(2,1)} %reshape.336), calls=%async_computation.3 | async-start | bytes 6291456 | tf_op jit(solution)/shard_map/all_to_all | solution.py:81
  598.7 29.4 %copy-start.5 = (f32[4,4]{1,0:T(4,128)S(1)}, f32[4,4]{1,0:T(4,128)}, u32[]{:S(2)}) copy-start(f32[4,4]{1,0:T(4,128)} %param.13) | copy-start | bytes 196
  621.0 46.8 %all-to-all-start.2 = ((bf16[8,2,98304]{2,1,0:T(2,128)(2,1)}), bf16[8,2,98304]{2,1,0:T(2,128)(2,1)}, u32[]{:S(2)}, u32[]{:S(2)}) async-start(bf16[8,2,98304]{2,1,0:T(2,128)(2,1)} %reshape.338), calls=%async_computation.2 | async-start | bytes 6291456 | tf_op jit(solution)/shard_map/all_to_all | solution.py:80
  625.4 523.0 %reduce-scatter.2.cloned.1.call-start = ((), (), s32[]{:S(2)}) async-start(), calls=%async_computation.5 | async-start | bytes 31457280 | tf_op jit(solution)/shard_map/reduce_scatter | solution.py:93
  691.8 22.3 %slice-start = ((s8[6291456]{0:T(1024)(128)(4,1)}), s8[2097152]{0:T(1024)(128)(4,1)S(1)}, s32[]{:S(2)}) async-start(s8[6291456]{0:T(1024)(128)(4,1)} %bitcast.183), calls=%async_computation.6 | async-start | bytes 4194304
  698.1 16.0 %slice-start.1 = ((s8[6291456]{0:T(1024)(128)(4,1)}), s8[4194304]{0:T(1024)(128)(4,1)S(1)}, s32[]{:S(2)}) async-start(s8[6291456]{0:T(1024)(128)(4,1)} %bitcast.183), calls=%async_computation.7 | async-start | bytes 8388608
  698.1 16.0 %copy-start.2 = (f32[128,3,512]{2,1,0:T(4,128)S(1)}, f32[128,3,512]{2,1,0:T(4,128)}, u32[]{:S(2)}) copy-start(f32[128,3,512]{2,1,0:T(4,128)} %copy.128) | copy-start | bytes 2359300
  698.1 16.0 %copy-start.3 = (f32[1,2,128,4,3,256]{5,3,4,1,2,0:T(4,128)S(1)}, f32[1,2,128,4,3,256]{5,3,4,1,2,0:T(4,128)}, u32[]{:S(2)}) copy-start(f32[1,2,128,4,3,256]{5,3,4,1,2,0:T(4,128)} %fusion.63) | copy-start | bytes 9437188
  731.7 19.7 %copy-start.4 = (f32[128,3,512]{2,0,1:T(8,128)S(1)}, f32[128,3,512]{2,0,1:T(8,128)}, u32[]{:S(2)}) copy-start(f32[128,3,512]{2,0,1:T(8,128)} %param.12) | copy-start | bytes 2359300
  1148.4 57.3 %copy-start.1 = (f32[2,512]{1,0:T(2,128)S(1)}, f32[2,512]{1,0:T(2,128)}, u32[]{:S(2)}) copy-start(f32[2,512]{1,0:T(2,128)} %param.11) | copy-start | bytes 12292
Sparse Core Ops, SparseCore 0:
  731.8 416.5 reduce-scatter.1
where the time goes:
time: 1220 us; the launch traced here: 1210 us
  waiting for transfers between devices  453 us (37%)
  matrix products  319 us (26%)
  local copies, waits for them, and re-layouts  181 us (15%)
  other arithmetic  169 us (14%)
  blocking collectives  56.8 us (5%)
  starting transfers between devices  18.8 us (2%)
  between operations  14.4 us (1%)
    reduce_scatter x1, waiting for transfers between devices, body(): lax.psum_scatter(quad_column[:, None, None, None, None, None] * force[Non...  395 us
    dot_general x1, matrix products, body(): lax.dot_general(fourier, backward, (((0, 2), (0, 1)), ((), ())), precisio...  167 us
    dot_general x1, matrix products, body(): jnp.einsum('cmk,qefhlk->cqmefhl', forward, tend, precision=lax.Precision....  85.2 us
    all_to_all x1, waiting for transfers between devices, body(): lax.all_to_all(even, 'band', split_axis=4, concat_axis=1, tiled=True)  45 us
    unnamed x25, local copies, waits for them, and re-layouts  43.3 us
    psum x1, blocking collectives, body(): total = lax.psum(change, ('node', 'band'))  42.1 us
    cos x1, other arithmetic, transform_tables(): cosine = jnp.cos(angle)  34.6 us
    another operation x1, other arithmetic, transform_tables(): slope_table = jnp.stack([-ratio * sine, -ratio * cosine], axis=0) * scale  33.7 us
  transfers between devices with their start and end apart: 5, of which 3 were waited for; matrix products, arithmetic and copies ran while one was open for 18% of the time, Pallas kernels for 0%

commit v1 on v0

v1 whole, which is shorter than its diff:
```python
import math

import jax
import jax.numpy as jnp
from jax import lax
from jax.sharding import PartitionSpec as P


def split_bf16(x):
    high = lax.reduce_precision(x, 8, 7)
    return high.astype(jnp.bfloat16), (x - high).astype(jnp.bfloat16)


def dft_table(parity, nband, local_modes, modes, points):
    fine = 32
    coarse = modes // fine
    column = lax.iota(jnp.int32, modes)
    pairs = local_modes // 2
    part = column // pairs % 2
    wave = column // local_modes * local_modes + column % pairs * 2 + parity
    unit = 2.0 * math.pi / points

    def angle(index):
        return (index % points).astype(jnp.float32) * unit

    big = angle(
        lax.iota(jnp.int32, coarse)[:, None] * fine * wave[None] + part[None] * (points // 4)
    )
    small = angle(lax.iota(jnp.int32, fine)[:, None] * wave[None])
    cos_big, sin_big = jnp.cos(big)[:, None], jnp.sin(big)[:, None]
    cos_small, sin_small = jnp.cos(small)[None], jnp.sin(small)[None]
    scale = 1.0 / math.sqrt(modes)
    slope_scale = wave.astype(jnp.float32) * (scale / modes)
    value = (cos_big * cos_small - sin_big * sin_small).reshape(modes, modes) * scale
    slope = -(sin_big * cos_small + cos_big * sin_small).reshape(modes, modes) * slope_scale
    return split_bf16(value), split_bf16(slope)


def mul(a, b, dims):
    return lax.dot_general(a, b, (dims, ((), ())), preferred_element_type=jnp.float32)


def body(state0, iterate, legendre, lat_weight, coriolis, damping, quadrature):
    spec = iterate[0]
    degrees = legendre.shape[2]
    half = degrees // 2
    local_modes, hemi = legendre.shape[:2]
    members, fields = spec.shape[2:4]
    nband = lax.axis_size("band")
    nnode = lax.axis_size("node")
    modes = local_modes * nband
    points = 2 * modes
    pairs = local_modes // 2
    lat_rows = hemi // nband
    node = lax.axis_index("node")
    band = lax.axis_index("band")
    tables = [dft_table(p, nband, local_modes, modes, points) for p in range(2)]
    cor = lax.dynamic_slice_in_dim(coriolis, band * lat_rows, lat_rows, 1)
    weight = lax.dynamic_slice_in_dim(lat_weight, band * lat_rows, lat_rows, 0)
    quad_row = lax.dynamic_slice_in_dim(quadrature, node, 1, 0)[0]
    diag = lax.dynamic_slice(quadrature, (node, node), (1, 1))[0, 0]
    is_even = lax.iota(jnp.int32, degrees) < half
    rate = damping[None, :, None]

    groups = 2
    ens = members // groups

    def synthesis(first):
        coeff = spec[:, :, first : first + ens].astype(jnp.bfloat16)
        coeff = coeff.transpose(1, 0, 3, 2, 4)
        zero = jnp.zeros((), jnp.bfloat16)
        rows = jnp.stack([jnp.where(is_even, coeff, zero), jnp.where(is_even, zero, coeff)], axis=1)
        rows = rows.reshape(local_modes, 4 * fields * ens, degrees)
        four = jnp.einsum("mrj,mlj->mrl", rows, legendre, preferred_element_type=jnp.float32)
        four = four.astype(jnp.bfloat16)
        four = four.reshape(pairs, 2, 2, 2, fields, ens, nband, lat_rows)
        four = four.transpose(6, 1, 3, 0, 2, 4, 5, 7)
        four = four.reshape(nband, 2, 2, pairs, 2 * fields * ens * lat_rows)
        return lax.all_to_all(four, "band", split_axis=0, concat_axis=0, tiled=True)

    def grid_step(four):
        shape = (modes, 2, fields, ens * lat_rows)
        parts = []
        for p in range(2):
            x = four[:, p].reshape(modes, -1)
            pair = []
            for high, low in tables[p]:
                dims = ((1,), (0,))
                pair.append((mul(high, x, dims) + mul(low, x, dims)).reshape(shape))
            parts.append(pair)
        tends = []
        for h in range(2):
            value, slope = (
                parts[0][v] + parts[1][v] if h == 0 else parts[0][v] - parts[1][v] for v in range(2)
            )
            hemis = []
            for s in range(2):
                val, slo = (
                    g[:, 0] + g[:, 1] if s == 0 else g[:, 0] - g[:, 1] for g in (value, slope)
                )
                c = jnp.tile(cor[s], ens)
                u, v, z = (val[:, f] for f in range(3))
                du, dv, dz = (slo[:, f] for f in range(3))
                hemis.append(
                    jnp.stack(
                        [-u * du + c * v - dz, -u * dv - c * u, -u * dz - (1.0 + z) * du], axis=1
                    )
                )
            tends.append(jnp.stack([hemis[0] + hemis[1], hemis[0] - hemis[1]], axis=1))
        scale = jnp.tile(weight, 2 * fields * ens)
        spectra = []
        for p in range(2):
            z = tends[0] + tends[1] if p == 0 else tends[0] - tends[1]
            zh, zl = split_bf16(z.reshape(modes, -1))
            high, low = tables[p][0]
            dims = ((0,), (0,))
            s = mul(high, zh, dims) + mul(high, zl, dims) + mul(low, zh, dims)
            spectra.append((s * scale).astype(jnp.bfloat16).reshape(nband, 2, pairs, -1))
        out = jnp.stack(spectra, axis=1)
        return lax.all_to_all(out, "band", split_axis=0, concat_axis=0, tiled=True)

    def analysis(out, first):
        out = out.reshape(nband, 2, 2, pairs, 2, fields, ens, lat_rows)
        out = out.transpose(3, 1, 4, 2, 5, 6, 0, 7)
        out = out.reshape(local_modes, 4 * fields * ens, hemi)
        both = jnp.einsum("mrl,mlj->mrj", out, legendre, preferred_element_type=jnp.float32)
        both = both.reshape(local_modes, 2, 2, fields, ens, degrees)
        nonlinear = jnp.where(is_even, both[:, 0], both[:, 1]).transpose(1, 0, 3, 2, 4)
        part = slice(first, first + ens)
        rest = nonlinear - rate * (spec[:, :, part] - state0[:, :, part])
        gathered = lax.all_gather(rest.astype(jnp.bfloat16), "node")
        mixed = sum(quad_row[p] * gathered[p].astype(jnp.float32) for p in range(nnode))
        return mixed

    received = [synthesis(g * ens) for g in range(groups)]
    spectra = [grid_step(r) for r in received]
    mixed = [analysis(s, g * ens) for g, s in enumerate(spectra)]
    mixed = jnp.concatenate(mixed, axis=2) - jnp.sum(quad_row) * (rate * state0)
    updated = (state0 + mixed + diag * rate * spec) / (1.0 + diag * rate)
    change = jnp.sum((updated - spec) ** 2, axis=(0, 1, 2, 4))
    base = jnp.sum(state0 * state0, axis=(0, 1, 2, 4))
    total = lax.psum(jnp.stack([change, base]), ("node", "band"))
    ratio = jnp.sqrt(total[0] / (total[1] + 1e-06))
    return (updated[None], ratio)


def solution(mesh):
    placed = (
        P(None, "band", None, None, None),
        P("node", None, "band", None, None, None),
        P("band", None, None),
        P(),
        P(),
        P("band", None, None),
        P(),
    )
    return jax.shard_map(
        body,
        mesh=mesh,
        in_specs=placed,
        out_specs=(P("node", None, "band", None, None, None), P()),
        check_vma=False,
    )
```

time: 1220 us -> 781 us (0.64)
  waiting for transfers between devices: 453 us -> 239 us
  matrix products: 319 us -> 173 us
  other arithmetic: 169 us -> 72.5 us
  local copies, waits for them, and re-layouts: 181 us -> 212 us
  blocking collectives: 56.8 us -> 38.3 us
    reduce_scatter x1 -> x0, waiting for transfers between devices: 395 us -> none  [body(): lax.psum_scatter(quad_column[:, None, None, None, None, None] * force[Non...]
    all_gather x0 -> x2, waiting for transfers between devices: none -> 217 us  [analysis(): gathered = lax.all_gather(rest.astype(jnp.bfloat16), 'node')]
    reshape x0 -> x16, local copies, waits for them, and re-layouts: none -> 153 us  [the longest x4 49.5 us: analysis(): out = out.reshape(nband, 2, 2, pairs, 2, fields, ens, lat_rows)]
    dot_general x6 -> x32, matrix products: 319 us -> 173 us  [the longest x28 67.6 us: mul(): lax.dot_general(a, b, (dims, ((), ())), preferred_element_type=jnp.float32)]
    another operation x2 -> x13, other arithmetic: 67 us -> 10.3 us  [the longest x8 3.97 us: grid_step(): jnp.stack([-u * du + c * v - dz, -u * dv - c * u, -u * dz - (1.0 + z) * d...]
    all_to_all x4 -> x0, local copies, waits for them, and re-layouts: 39.5 us -> none  [the longest x2 21.6 us: body(): lax.all_to_all(symmetric, 'band', split_axis=1, concat_axis=4, tiled=True)]
    all_to_all x4, waiting for transfers between devices: 58.4 us -> 20.7 us  [the longest x2 15.6 us: synthesis(): return lax.all_to_all(four, 'band', split_axis=0, concat_axis=0, tiled=True)]
    cos x1, other arithmetic: 34.6 us -> 2.08 us  [dft_table(): cos_big, sin_big = (jnp.cos(big)[:, None], jnp.sin(big)[:, None])]
  transfers between devices with their start and end apart: 5 -> 6, of which waited for: 3 -> 4; matrix products, arithmetic and copies ran while one was open for 18% -> 28% of each run, Pallas kernels for 0% -> 0%
where the time goes in v1:
time: 781 us; the launch traced here: 770 us
  waiting for transfers between devices  239 us (31%)
  local copies, waits for them, and re-layouts  212 us (27%)
  matrix products  173 us (22%)
  other arithmetic  72.5 us (9%)
  blocking collectives  38.3 us (5%)
  starting transfers between devices  19.7 us (3%)
  between operations  15.3 us (2%)
    all_gather x2, waiting for transfers between devices, analysis(): gathered = lax.all_gather(rest.astype(jnp.bfloat16), 'node')  217 us
    dot_general x28, matrix products, mul(): lax.dot_general(a, b, (dims, ((), ())), preferred_element_type=jnp.float32)  67.6 us
    dot_general x2, matrix products, synthesis(): jnp.einsum('mrj,mlj->mrl', rows, legendre, preferred_element_type=jnp.flo...  54.6 us
    dot_general x2, matrix products, analysis(): jnp.einsum('mrl,mlj->mrj', out, legendre, preferred_element_type=jnp.floa...  51.1 us
    reshape x4, local copies, waits for them, and re-layouts, analysis(): out = out.reshape(nband, 2, 2, pairs, 2, fields, ens, lat_rows)  49.5 us
    reshape x4, local copies, waits for them, and re-layouts, synthesis(): four = four.reshape(pairs, 2, 2, 2, fields, ens, nband, lat_rows)  38.5 us
    psum x1, blocking collectives, body(): total = lax.psum(jnp.stack([change, base]), ('node', 'band'))  38.3 us
    unnamed x83, local copies, waits for them, and re-layouts  24.9 us
  transfers between devices with their start and end apart: 6, of which 4 were waited for; matrix products, arithmetic and copies ran while one was open for 28% of the time, Pallas kernels for 0%

profile of v1, /device:TPU:0, one launch (start us, length us, event | category | flops | bytes accessed | tf_op | source)
XLA Modules:
  0.0 769.7 jit_solution(12251660246669993909)
XLA Ops:
  25.5 27.3 %convolution_convert_fusion = bf16[128,24,512]{2,1,0:T(8,128)(2,1)} fusion(bf16[128,24,512]{2,1,0:T(8,128)(2,1)S(1)} %reshape.1694, bf16[128,512,512]{2,1,0:T(8,128)(2,1)} %param.9), kind=kOutput, calls=%fused_computation.75 | convolution fusion | flops 1612185600 | bytes 73400320 | tf_op jit(solution)/shard_map/mrj,mlj->mrl/dot_general | solution.py:74
  52.8 8.9 %reshape.1695 = bf16[64,2,2,2,3,2,8,64]{7,6,5,4,3,2,1,0:T(8,128)(2,1)} reshape(bf16[128,24,512]{2,1,0:T(8,128)(2,1)} %convolution_convert_fusion) | data formatting | bytes 6291456 | tf_op jit(solution)/shard_map/reshape | solution.py:76
  61.7 10.4 %copy.92 = bf16[64,2,2,2,3,2,8,64]{7,5,4,2,0,3,1,6:T(2,128)(2,1)} copy(bf16[64,2,2,2,3,2,8,64]{7,6,5,4,3,2,1,0:T(8,128)(2,1)} %reshape.1695) | data formatting | bytes 6291456 | tf_op jit(solution)/shard_map/reshape | solution.py:76
  72.0 12.2 %reshape.1696 = bf16[8,2,2,64,768]{4,3,2,1,0:T(8,128)(2,1)} reshape(bf16[8,2,2,64,2,3,2,64]{7,6,5,4,3,2,1,0:T(2,128)(2,1)} %bitcast.278) | data formatting | bytes 6291456 | tf_op jit(solution)/shard_map/reshape | solution.py:78
  99.7 27.3 %convolution_convert_fusion.1 = bf16[128,24,512]{2,1,0:T(8,128)(2,1)} fusion(bf16[128,24,512]{2,1,0:T(8,128)(2,1)S(1)} %reshape.1688, bf16[128,512,512]{2,1,0:T(8,128)(2,1)} %param.9), kind=kOutput, calls=%fused_computation.76 | convolution fusion | flops 1612185600 | bytes 73400320 | tf_op jit(solution)/shard_map/mrj,mlj->mrl/dot_general | solution.py:74
  127.0 8.9 %reshape.1689 = bf16[64,2,2,2,3,2,8,64]{7,6,5,4,3,2,1,0:T(8,128)(2,1)} reshape(bf16[128,24,512]{2,1,0:T(8,128)(2,1)} %convolution_convert_fusion.1) | data formatting | bytes 6291456 | tf_op jit(solution)/shard_map/reshape | solution.py:76
  135.9 10.4 %copy.94 = bf16[64,2,2,2,3,2,8,64]{7,5,4,2,0,3,1,6:T(2,128)(2,1)} copy(bf16[64,2,2,2,3,2,8,64]{7,6,5,4,3,2,1,0:T(8,128)(2,1)} %reshape.1689) | data formatting | bytes 6291456 | tf_op jit(solution)/shard_map/reshape | solution.py:76
  146.2 12.2 %reshape.1690 = bf16[8,2,2,64,768]{4,3,2,1,0:T(8,128)(2,1)} reshape(bf16[8,2,2,64,2,3,2,64]{7,6,5,4,3,2,1,0:T(2,128)(2,1)} %bitcast.279) | data formatting | bytes 6291456 | tf_op jit(solution)/shard_map/reshape | solution.py:78
  172.7 8.2 %fusion.5 = (bf16[32,32,1024]{2,1,0:T(8,128)(2,1)}, bf16[32,32,1024]{2,1,0:T(8,128)(2,1)}, bf16[32,32,1024]{2,1,0:T(8,128)(2,1)S(1)}, bf16[32,32,1024]{2,1,0:T(8...) fusion(f32[1024]{0:T(1024)S(1)} %convert_multiply_fusion.1, ...), kind=kLoop, calls=%fused_computation.29 | loop fusion | flops 35651584 | bytes 17833984 | tf_op jit(solution)/shard_map/convert_element_type | solution.py:11
  192.9 15.6 %all-to-all-done = bf16[8,2,2,64,768]{4,3,2,1,0:T(8,128)(2,1)} async-done(((bf16[8,2,2,64,768]{4,3,2,1,0:T(8,128)(2,1)}), bf16[8,2,2,64,768]{4,3,2,1,0:T(8,128)(2,1)}, u32[]{:S(2)}, u32[]{:S(2)}) %all-to-all-start) | async-done | bytes 3145760 | tf_op jit(solution)/shard_map/all_to_all | solution.py:79
  307.0 12.2 %reshape.1697 = bf16[8,2,2,64,2,3,2,64]{7,6,5,4,3,2,1,0:T(2,128)(2,1)} reshape(bf16[8,2,2,64,768]{4,3,2,1,0:T(8,128)(2,1)} %all-to-all-done.3) | data formatting | bytes 6291456 | tf_op jit(solution)/shard_map/reshape | solution.py:123
  319.3 12.7 %copy.91 = bf16[8,2,2,64,2,3,2,64]{7,0,6,5,2,4,1,3:T(8,128)(2,1)} copy(bf16[8,2,2,64,2,3,2,64]{7,6,5,4,3,2,1,0:T(2,128)(2,1)} %reshape.1697) | data formatting | bytes 6291456 | tf_op jit(solution)/shard_map/reshape | solution.py:123
  331.9 8.0 %reshape.1698 = bf16[128,24,512]{2,1,0:T(8,128)(2,1)S(1)} reshape(bf16[64,2,2,2,3,2,8,64]{7,6,5,4,3,2,1,0:T(8,128)(2,1)} %bitcast.280) | data formatting | bytes 6291456 | tf_op jit(solution)/shard_map/reshape | solution.py:125
  340.0 25.5 %fusion.165 = f32[128,24,512]{2,1,0:T(8,128)} fusion(bf16[128,24,512]{2,1,0:T(8,128)(2,1)S(1)} %reshape.1698, bf16[128,512,512]{2,1,0:T(8,128)(2,1)} %param.9), kind=kOutput, calls=%fused_computation.319 | convolution fusion | flops 1610612736 | bytes 76546048 | tf_op jit(solution)/shard_map/mrl,mlj->mrj/dot_general | solution.py:126
  365.5 8.2 %reshape.1699 = f32[128,2,2,3,2,512]{5,4,3,2,1,0:T(2,128)} reshape(f32[128,24,512]{2,1,0:T(8,128)} %fusion.165) | data formatting | bytes 12582912 | tf_op jit(solution)/shard_map/reshape | solution.py:127
  381.5 12.0 %reshape.1691 = bf16[8,2,2,64,2,3,2,64]{7,6,5,4,3,2,1,0:T(2,128)(2,1)} reshape(bf16[8,2,2,64,768]{4,3,2,1,0:T(8,128)(2,1)} %all-to-all-done.1) | data formatting | bytes 6291456 | tf_op jit(solution)/shard_map/reshape | solution.py:123
  393.5 12.7 %copy.93 = bf16[8,2,2,64,2,3,2,64]{7,0,6,5,2,4,1,3:T(8,128)(2,1)} copy(bf16[8,2,2,64,2,3,2,64]{7,6,5,4,3,2,1,0:T(2,128)(2,1)} %reshape.1691) | data formatting | bytes 6291456 | tf_op jit(solution)/shard_map/reshape | solution.py:123
  414.1 25.5 %fusion.156 = f32[128,24,512]{2,1,0:T(8,128)} fusion(bf16[128,24,512]{2,1,0:T(8,128)(2,1)S(1)} %reshape.1692, bf16[128,512,512]{2,1,0:T(8,128)(2,1)} %param.9), kind=kOutput, calls=%fused_computation.310 | convolution fusion | flops 1610612736 | bytes 76546048 | tf_op jit(solution)/shard_map/mrl,mlj->mrj/dot_general | solution.py:126
  439.7 8.6 %reshape.1693 = f32[128,2,2,3,2,512]{5,4,3,2,1,0:T(2,128)} reshape(f32[128,24,512]{2,1,0:T(8,128)} %fusion.156) | data formatting | bytes 12582912 | tf_op jit(solution)/shard_map/reshape | solution.py:127
  455.2 8.3 %fusion.16 = (bf16[2,128,2,3,512]{4,1,3,2,0:T(8,128)(2,1)}, bf16[2,128,2,3,512]{4,1,3,2,0:T(8,128)(2,1)}) fusion(f32[2,128,4,3,512]{4,1,3,2,0:T(8,128)} %copy.53, f32[128,1,2,3,2,512]{5,4,3,2,1,0:T(2,128)} %get-tuple-element.17, f32[128,1,2,3,2,512]{5,4,3,2,1,0:T(2,128)S(1)} %get-tuple-element.16, f32[2,128,4,3,512]{4,1,3,2,0:T(8,128)S(1)} %bitcast.277, ...), kind=kLoop, calls=%fused_computation.46 | loop fusion | flops 7864320 | bytes 29098496 | tf_op jit(solution)/shard_map/convert_element_type | solution.py:131
  472.5 108.7 %all-gather.5.cloned.1.call-done = bf16[8,128,2,3,512]{4,1,3,2,0:T(8,128)(2,1)} async-done(((bf16[2,128,2,3,512]{4,1,3,2,0:T(8,128)(2,1)}), bf16[8,128,2,3,512]{4,1,3,2,0:T(8,128)(2,1)}) %all-gather.5.cloned.1.call-update) | async-done | bytes 6291472 | tf_op jit(solution)/shard_map/all_gather | solution.py:131
  587.9 108.5 %all-gather.7.cloned.1.call-done = bf16[8,128,2,3,512]{4,1,3,2,0:T(8,128)(2,1)} async-done(((bf16[2,128,2,3,512]{4,1,3,2,0:T(8,128)(2,1)}), bf16[8,128,2,3,512]{4,1,3,2,0:T(8,128)(2,1)}) %all-gather.7.cloned.1.call-update) | async-done | bytes 6291472 | tf_op jit(solution)/shard_map/all_gather | solution.py:131
  703.2 13.6 %multiply_reduce_fusion.1 = (f32[3]{0:T(128)S(1)}, f32[2,128,4,3,512]{4,1,3,2,0:T(8,128)S(1)}) fusion(f32[1,2,128,4,3,512]{5,3,4,2,1,0:T(4,128)} %param.8, f32[128,3,512]{2,0,1:T(8,128)S(1)} %copy-done.13, f32[128,3,512]{2,0,1:T(8,128)S(1)} %copy-done.14, f32[128,3,512]{2,0,1:T(8,128)S(1)} %copy-done.12, f32[]{:T(128)} %get-tuple-element.6, ...), kind=kLoop, calls=%fused_computation.10 | loop fusion | flops 17301500 | bytes 27525136 | tf_op jit(solution)/shard_map/reduce_sum | solution.py:140
  723.5 38.3 %psum.7 = f32[2,3]{1,0:T(2,128)S(1)} all-reduce(f32[2,3]{1,0:T(2,128)S(1)} %pad_maximum_fusion.16), channel_id=1, replica_groups=mesh['node'=4,'band'=8] {'node','band'}, use_global_device_ids=true, to_apply=%region_3.4 | all-reduce | flops 6 | bytes 48 | tf_op jit(solution)/shard_map/psum | solution.py:142
  (184 shorter events, 210.1 us)
Async XLA Ops:
  7.2 82.5 %copy-start = (f32[2,512]{1,0:T(2,128)S(1)}, f32[2,512]{1,0:T(2,128)}, u32[]{:S(2)}) copy-start(f32[2,512]{1,0:T(2,128)} %param.11) | copy-start | bytes 12292
  84.2 6.6 copy-start.8
  84.2 81.6 %all-to-all-start.2 = ((bf16[8,2,2,64,768]{4,3,2,1,0:T(8,128)(2,1)}), bf16[8,2,2,64,768]{4,3,2,1,0:T(8,128)(2,1)}, u32[]{:S(2)}, u32[]{:S(2)}) async-start(bf16[8,2,2,64,768]{4,3,2,1,0:T(8,128)(2,1)} %reshape.1696), calls=%async_computation.2 | async-start | bytes 6291456 | tf_op jit(solution)/shard_map/all_to_all | solution.py:79
  165.8 42.7 %all-to-all-start = ((bf16[8,2,2,64,768]{4,3,2,1,0:T(8,128)(2,1)}), bf16[8,2,2,64,768]{4,3,2,1,0:T(8,128)(2,1)}, u32[]{:S(2)}, u32[]{:S(2)}) async-start(bf16[8,2,2,64,768]{4,3,2,1,0:T(8,128)(2,1)} %reshape.1690), calls=%async_computation | async-start | bytes 6291456 | tf_op jit(solution)/shard_map/all_to_all | solution.py:79
  181.0 4.8 copy-start.26
  181.0 8.4 %copy-start.19 = (bf16[32,32,1024]{2,1,0:T(8,128)(2,1)}, bf16[32,32,1024]{2,1,0:T(8,128)(2,1)S(1)}, u32[]{:S(2)}) copy-start(bf16[32,32,1024]{2,1,0:T(8,128)(2,1)S(1)} %get-tuple-element.116) | copy-start | bytes 6291460
  210.8 15.3 %copy-start.5 = (bf16[8,1,2,64,768]{4,3,2,1,0:T(8,128)(2,1)}, bf16[8,1,2,64,768]{4,3,2,1,0:T(8,128)(2,1)S(1)}, u32[]{:S(2)}) copy-start(bf16[8,1,2,64,768]{4,3,2,1,0:T(8,128)(2,1)S(1)} %get-tuple-element.69) | copy-start | bytes 4718596
  259.8 42.7 %all-to-all-start.3 = ((bf16[8,2,2,64,768]{4,3,2,1,0:T(8,128)(2,1)}), bf16[8,2,2,64,768]{4,3,2,1,0:T(8,128)(2,1)}, u32[]{:S(2)}, u32[]{:S(2)}) async-start(bf16[8,2,2,64,768]{4,3,2,1,0:T(8,128)(2,1)} %pad_maximum_fusion.7), calls=%async_computation.3 | async-start | bytes 6291456 | tf_op jit(solution)/shard_map/all_to_all | solution.py:120
  264.6 5.2 copy-start.4
  264.6 5.2 copy-start.6
  264.6 5.2 copy-start.16
  302.5 79.0 %all-to-all-start.1 = ((bf16[8,2,2,64,768]{4,3,2,1,0:T(8,128)(2,1)}), bf16[8,2,2,64,768]{4,3,2,1,0:T(8,128)(2,1)}, u32[]{:S(2)}, u32[]{:S(2)}) async-start(bf16[8,2,2,64,768]{4,3,2,1,0:T(8,128)(2,1)} %pad_maximum_fusion.3), calls=%async_computation.1 | async-start | bytes 6291456 | tf_op jit(solution)/shard_map/all_to_all | solution.py:120
  307.0 274.3 %all-gather.5.cloned.1.call-start = ((), (), s32[]{:S(2)}) async-start(), calls=%async_computation.4 | async-start | bytes 7864320 | tf_op jit(solution)/shard_map/all_gather | solution.py:131
  439.7 15.4 %slice-start = ((s8[6291456]{0:T(1024)(128)(4,1)}), s8[2097152]{0:T(1024)(128)(4,1)S(1)}, s32[]{:S(2)}) async-start(s8[6291456]{0:T(1024)(128)(4,1)} %bitcast.275), calls=%async_computation.6 | async-start | bytes 4194304
  448.3 6.9 slice-start.1
  448.3 6.8 copy-start.9
  448.3 6.8 copy-start.10
  448.3 6.8 copy-start.11
  448.3 6.8 copy-start.33
  463.5 232.9 %all-gather.7.cloned.1.call-start = ((), (), s32[]{:S(2)}) async-start(), calls=%async_computation.5 | async-start | bytes 7864320 | tf_op jit(solution)/shard_map/all_gather | solution.py:131
  696.4 6.7 copy-start.12
  696.4 6.8 copy-start.13
  696.4 6.8 copy-start.14
  716.8 45.6 %copy-start.1 = (f32[2,512]{1,0:T(2,128)S(1)}, f32[2,512]{1,0:T(2,128)}, u32[]{:S(2)}) copy-start(f32[2,512]{1,0:T(2,128)} %param.11) | copy-start | bytes 12292
  (22 other events, 59.8 us)
Sparse Core Ops, SparseCore 0:
  463.6 117.6 all-gather.4
  582.8 113.5 all-gather.6
